TPU v7x, 256 devices: a whole 4x4x8 slice. The times are simulated.
256 devices in a mesh: row: 16 (over z, core), col: 16 (over y, x).
Axes of the slice: x: 4, y: 4, z: 8, core: 2. Of those that a mesh axis runs over, the one named last changes fastest.
Arguments:
- front_blocks: bfloat16 [64, 5, 512, 512], P('row'), may hold values from -0.125 to 0.125
- block_cols: int32 [64, 5], P('row'), may hold values from 0 to 63, as said below
- samples: bfloat16 [32768, 1024], P('row', 'col'), may hold values from -6 to 6
- sketch_matrix: bfloat16 [1024, 256], replicated, may hold values from -0.1875 to 0.1875
Outputs:
- leaf_bases: bfloat16 [32768, 256], P('row')
- top_transfers: bfloat16 [1024, 256], P('row')
Inputs may be any that keep to these rules, and one draw needn't show every extreme that they name: `block_cols`: each row lists 5 different block columns; the first is the row's own index, the second lies in the other half of the 64 block columns (its index differs in the highest bit).
All inputs are finite; a program needn't handle non-finite values.
Results may differ from a plain program's by a relative error of at most 0.035.
Values may be sent and summed in bfloat16 or wider, within the bound.
No kernel may reach another device: no remote copies, remote signals or barrier semaphores. Data moves between devices by JAX's collectives and lax.ppermute only.
A program may use at most 128 MiB of HBM per device.

v0:
```python
import math
import jax
import jax.numpy as jnp
from jax import lax
from jax.sharding import PartitionSpec as P


def partner_2(value, axis, stride):
    mask = 2**stride
    pairs = [(source, source ^ mask) for source in range(lax.axis_size(axis))]
    return lax.ppermute(value, axis, pairs)


def cholqr(sketch):
    highest = lax.Precision.HIGHEST
    gram_matrix = jnp.dot(sketch.T, sketch, precision=highest)
    low_factor = jnp.linalg.cholesky(gram_matrix)
    identity = jnp.eye(sketch.shape[1], dtype=sketch.dtype)
    low_inverse = jax.scipy.linalg.solve_triangular(low_factor, identity, lower=True)
    ortho_basis = jnp.dot(sketch, low_inverse.T, precision=highest)
    return (ortho_basis * math.sqrt(sketch.shape[0])).astype(jnp.bfloat16)


def off_products(all_sketched, front_blocks, block_cols, leaf_ids, top_level):
    leaf_total = all_sketched.shape[0] // front_blocks.shape[2]
    gathered_blocks = all_sketched.reshape(
        leaf_total, front_blocks.shape[2], all_sketched.shape[1]
    )[block_cols]
    products = jnp.einsum(
        "nkab,nkbc->nkac", front_blocks, gathered_blocks, preferred_element_type=jnp.float32
    )
    level_ids = jnp.arange(top_level, dtype=jnp.int32)
    outside = (
        jnp.right_shift(leaf_ids[:, None, None], level_ids[None, :, None])
        != jnp.right_shift(block_cols[:, None, :], level_ids[None, :, None])
    ).astype(jnp.float32)
    return jnp.einsum("nlk,nkac->nlac", outside, products, precision=lax.Precision.HIGHEST).astype(
        jnp.bfloat16
    )


def shards(front_blocks, block_cols, samples, sketch_matrix):
    leaf_dev = front_blocks.shape[0]
    leaf_size = front_blocks.shape[2]
    rank_size = sketch_matrix.shape[1]
    cols_dev = samples.shape[1]
    size_rows = lax.axis_size("row")
    row_index = lax.axis_index("row")
    leaf_total = leaf_dev * size_rows
    top_level = leaf_total.bit_length() - 1
    local_levels = leaf_dev.bit_length() - 1
    leaf_ids = row_index * leaf_dev + jnp.arange(leaf_dev, dtype=jnp.int32)
    local_rows = lax.dynamic_slice_in_dim(
        sketch_matrix, lax.axis_index("col") * cols_dev, cols_dev, 0
    )
    partial_sum = jnp.dot(samples, local_rows, preferred_element_type=jnp.float32)
    sketched = lax.psum(partial_sum.astype(jnp.bfloat16), "col")
    all_sketched = lax.all_gather(sketched, "row", axis=0, tiled=True)
    off_samples = off_products(all_sketched, front_blocks, block_cols, leaf_ids, top_level)
    leaf_basis = jax.vmap(cholqr)(off_samples[:, 0].astype(jnp.float32))
    carried = jnp.einsum(
        "nar,nlac->nlrc", leaf_basis, off_samples[:, 1:], preferred_element_type=jnp.float32
    )
    carried = (carried * (1.0 / math.sqrt(leaf_size))).astype(jnp.bfloat16)
    scale_pair = 1.0 / math.sqrt(2 * rank_size)
    transfer = None
    for tree_level in range(1, top_level):
        if carried.shape[0] >= 2:
            node_count = carried.shape[0] // 2
            paired = carried.reshape(node_count, 2, carried.shape[1], rank_size, rank_size)
            stacked = jnp.concatenate([paired[:, 0], paired[:, 1]], axis=2)
        else:
            swap_bit = tree_level - local_levels - 1
            is_left = jnp.right_shift(row_index, swap_bit) % 2 == 0
            partner = partner_2(carried, "row", swap_bit)
            left_part = jnp.where(is_left, carried, partner)
            right_part = jnp.where(is_left, partner, carried)
            stacked = jnp.concatenate([left_part, right_part], axis=2)
        transfer = jax.vmap(cholqr)(stacked[:, 0].astype(jnp.float32))
        if tree_level < top_level - 1:
            moved = jnp.einsum(
                "npr,nlpc->nlrc", transfer, stacked[:, 1:], preferred_element_type=jnp.float32
            )
            carried = (moved * scale_pair).astype(jnp.bfloat16)
    out_rows = 4 * rank_size // size_rows
    offset = row_index % (size_rows // 2) * out_rows
    top_rows = lax.dynamic_slice_in_dim(transfer[0], offset, out_rows, 0)
    return (leaf_basis.reshape(leaf_dev * leaf_size, rank_size), top_rows)


def solution(mesh):
    placed = (P("row", None, None, None), P("row", None), P("row", "col"), P())
    return jax.shard_map(
        shards,
        mesh=mesh,
        in_specs=placed,
        out_specs=(P("row", None), P("row", None)),
        check_vma=False,
    )
```

profile of v0, /device:TPU:1, one launch (start us, length us, event | category | flops | bytes accessed | tf_op | source)
XLA Modules:
  0.0 963.2 jit_solution(16113320740704673089)
XLA Ops:
  8.2 2.4 fusion.2
  10.7 100.7 %all-reduce.5.cloned.1.call-done = bf16[2048,256]{0,1:T(8,128)(2,1)} async-done(((bf16[2048,256]{0,1:T(8,128)(2,1)}), bf16[2048,256]{0,1:T(8,128)(2,1)}) %all-reduce.5.cloned.1.call-update) | async-done | bytes 1048592 | tf_op jit(solution)/shard_map/psum | solution.py:57
  111.8 98.0 %all-gather.2.cloned.1.call-done = bf16[32768,256]{0,1:T(8,128)(2,1)} async-done(((bf16[2048,256]{0,1:T(8,128)(2,1)}), bf16[32768,256]{0,1:T(8,128)(2,1)}) %all-gather.2.cloned.1.call-update) | async-done | bytes 16777232 | tf_op jit(solution)/shard_map/all_gather | solution.py:58
  209.8 22.4 %copy.112 = bf16[32768,256]{1,0:T(8,128)(2,1)} copy(bf16[32768,256]{0,1:T(8,128)(2,1)} %all-gather.2.cloned.1.call-done) | data formatting | bytes 33554432 | tf_op jit(solution)/shard_map/reshape | solution.py:26
  232.2 9.9 %gather_fusion = bf16[20,512,256]{2,1,0:T(8,128)(2,1)} fusion(bf16[64,512,256]{2,1,0:T(8,128)(2,1)} %bitcast.432, s32[1024]{0:T(1024)S(1)} %pad_clamp_fusion), kind=kCustom, calls=%fused_computation | custom fusion | bytes 10485840 | tf_op jit(solution)/shard_map/gather | solution.py:26
  242.0 12.5 %convolution_bitcast_fusion = f32[4,5,512,256]{2,3,1,0:T(8,128)} fusion(bf16[4,5,512,256]{3,2,1,0:T(8,128)(2,1)} %bitcast.433, bf16[4,5,512,512]{3,2,1,0:T(8,128)(2,1)} %param.7), kind=kOutput, calls=%fused_computation.17 | convolution fusion | flops 2684354560 | bytes 26214400 | tf_op jit(solution)/shard_map/nkab,nkbc->nkac/dot_general | solution.py:29
  254.6 17.1 %copy.63 = f32[4,5,512,256]{3,1,2,0:T(8,128)} copy(f32[4,5,512,256]{2,3,1,0:T(8,128)} %convolution_bitcast_fusion) | data formatting | bytes 20971520 | tf_op jit(solution)/shard_map/nkab,nkbc->nkac/dot_general | solution.py:29
  271.7 11.9 %convolution_convert_fusion = bf16[4,6,512,256]{3,1,2,0:T(8,128)(2,1)S(1)} fusion(f32[4,5,512,256]{3,1,2,0:T(8,128)} %copy.63, s32[4,5]{1,0:T(4,128)S(1)} %copy-done.11, s32[4,6]{1,0:T(4,128)S(1)} %iota_shift-right-arithmetic_fusion), kind=kOutput, calls=%fused_computation.13 | convolution fusion | flops 191889648 | bytes 16777392 | tf_op jit(solution)/shard_map/nlk,nkac->nlac/dot_general | solution.py:37
  283.6 3.2 copy-done.2
  286.8 1.4 slice.234
  288.3 9.4 slice.235
  299.7 46.9 %custom-call.47 = f32[4,128,128]{2,1,0:T(8,128)S(1)} custom-call(f32[4,128,128]{2,1,0:T(8,128)S(1)} %cholesky.577), custom_call_target="Cholesky" | custom-call | tf_op jit(solution)/shard_map/vmap(jit(cholesky))/cholesky | solution.py:17
  346.7 39.3 %custom-call.48 = f32[4,1,128,128]{2,3,1,0:T(8,128)S(1)} custom-call(f32[4,1,128,128]{3,2,1,0:T(8,128)S(1)} %select_bitcast_fusion), custom_call_target="InvertDiagBlocksLowerTriangular" | custom-call | tf_op jit(solution)/shard_map/vmap(jit(cholesky))/cholesky | solution.py:17
  386.1 1.4 constant_dynamic-update-slice_fusion.7
  387.4 1.6 convolution_subtract_fusion.2
  389.1 59.6 %custom-call.49 = f32[4,128,128]{2,1,0:T(8,128)S(1)} custom-call(f32[4,128,128]{2,1,0:T(8,128)S(1)} %convolution_subtract_fusion.2), custom_call_target="Cholesky" | custom-call | tf_op jit(solution)/shard_map/vmap(jit(cholesky))/cholesky | solution.py:17
  449.2 5.3 while.10
  449.8 2.1 bitcast_dynamic-update-slice_fusion.16
  452.4 2.1 bitcast_dynamic-update-slice_fusion.16
  454.5 79.4 %custom-call.50 = f32[4,2,128,128]{2,3,1,0:T(8,128)S(1)} custom-call(f32[4,2,128,128]{3,2,1,0:T(8,128)} %bitcast.451), custom_call_target="InvertDiagBlocksLowerTriangular" | custom-call | tf_op jit(solution)/shard_map/vmap(jit(_solve_triangular))/triangular_solve | solution.py:19
  535.8 2.7 multiply_convert_fusion.2
  538.5 5.7 multiply_convert_fusion
  545.9 2.1 copy.76
  550.6 24.3 %custom-call.51 = f32[2,128,128]{2,1,0:T(8,128)S(1)} custom-call(f32[2,128,128]{2,1,0:T(8,128)} %cholesky.580), custom_call_target="Cholesky" | custom-call | tf_op jit(solution)/shard_map/vmap(jit(cholesky))/cholesky | solution.py:17
  574.9 1.4 select_bitcast_fusion.1
  577.1 21.5 %custom-call.52 = f32[2,1,128,128]{2,3,1,0:T(8,128)} custom-call(f32[2,1,128,128]{3,2,1,0:T(8,128)} %select_bitcast_fusion.1), custom_call_target="InvertDiagBlocksLowerTriangular" | custom-call | tf_op jit(solution)/shard_map/vmap(jit(cholesky))/cholesky | solution.py:17
  598.6 1.9 constant_dynamic-update-slice_fusion.5
  600.6 1.9 convolution_subtract_fusion.3
  602.5 24.9 %custom-call.53 = f32[2,128,128]{2,1,0:T(8,128)} custom-call(f32[2,128,128]{2,1,0:T(8,128)} %convolution_subtract_fusion.3), custom_call_target="Cholesky" | custom-call | tf_op jit(solution)/shard_map/vmap(jit(cholesky))/cholesky | solution.py:17
  627.4 1.6 select_reduce_fusion.2
  629.2 2.0 select_select_fusion.1
  631.2 8.3 while.11
  632.4 3.0 bitcast_dynamic-update-slice_fusion.17
  636.6 2.9 bitcast_dynamic-update-slice_fusion.17
  639.6 40.9 %custom-call.54 = f32[2,2,128,128]{2,3,1,0:T(8,128)} custom-call(f32[2,2,128,128]{3,2,1,0:T(8,128)} %bitcast.452), custom_call_target="InvertDiagBlocksLowerTriangular" | custom-call | tf_op jit(solution)/shard_map/vmap(jit(_solve_triangular))/triangular_solve | solution.py:19
  681.8 1.3 convolution_subtract_fusion.1
  686.5 11.7 %custom-call.67 = f32[1,128,128]{2,1,0:T(8,128)S(1)} custom-call(f32[1,128,128]{2,1,0:T(8,128)S(1)} %cholesky.583), custom_call_target="Cholesky" | custom-call | tf_op jit(solution)/shard_map/vmap(jit(cholesky))/cholesky | solution.py:17
  698.3 9.8 %custom-call.68 = f32[1,1,128,128]{2,3,1,0:T(8,128)S(1)} custom-call(f32[1,1,128,128]{3,2,1,0:T(8,128)S(1)} %get-tuple-element.143), custom_call_target="InvertDiagBlocksLowerTriangular" | custom-call | tf_op jit(solution)/shard_map/vmap(jit(cholesky))/cholesky | solution.py:17
  708.6 12.1 %custom-call.69 = f32[1,128,128]{2,1,0:T(8,128)S(1)} custom-call(f32[1,128,128]{2,1,0:T(8,128)S(1)} %fusion.34), custom_call_target="Cholesky" | custom-call | tf_op jit(solution)/shard_map/vmap(jit(cholesky))/cholesky | solution.py:17
  723.5 4.1 while.12
  724.1 1.4 bitcast_dynamic-update-slice_fusion.18
  726.2 1.4 bitcast_dynamic-update-slice_fusion.18
  727.6 19.7 %custom-call.70 = f32[1,2,128,128]{2,3,1,0:T(8,128)S(1)} custom-call(f32[1,2,128,128]{3,2,1,0:T(8,128)S(1)} %bitcast.448), custom_call_target="InvertDiagBlocksLowerTriangular" | custom-call | tf_op jit(solution)/shard_map/vmap(jit(_solve_triangular))/triangular_solve | solution.py:19
  749.4 1.5 collective-permute-done
  751.4 11.7 %custom-call.71 = f32[1,128,128]{2,1,0:T(8,128)S(1)} custom-call(f32[1,128,128]{2,1,0:T(8,128)S(1)} %cholesky.586), custom_call_target="Cholesky" | custom-call | tf_op jit(solution)/shard_map/vmap(jit(cholesky))/cholesky | solution.py:17
  763.2 9.8 %custom-call.72 = f32[1,1,128,128]{2,3,1,0:T(8,128)S(1)} custom-call(f32[1,1,128,128]{3,2,1,0:T(8,128)S(1)} %get-tuple-element.139), custom_call_target="InvertDiagBlocksLowerTriangular" | custom-call | tf_op jit(solution)/shard_map/vmap(jit(cholesky))/cholesky | solution.py:17
  773.5 11.7 %custom-call.73 = f32[1,128,128]{2,1,0:T(8,128)S(1)} custom-call(f32[1,128,128]{2,1,0:T(8,128)S(1)} %fusion.35), custom_call_target="Cholesky" | custom-call | tf_op jit(solution)/shard_map/vmap(jit(cholesky))/cholesky | solution.py:17
  787.9 4.2 while.13
  792.2 19.7 %custom-call.74 = f32[1,2,128,128]{2,3,1,0:T(8,128)S(1)} custom-call(f32[1,2,128,128]{3,2,1,0:T(8,128)S(1)} %bitcast.449), custom_call_target="InvertDiagBlocksLowerTriangular" | custom-call | tf_op jit(solution)/shard_map/vmap(jit(_solve_triangular))/triangular_solve | solution.py:19
  813.6 7.6 collective-permute-done.1
  821.8 11.7 %custom-call.75 = f32[1,128,128]{2,1,0:T(8,128)S(1)} custom-call(f32[1,128,128]{2,1,0:T(8,128)S(1)} %cholesky.589), custom_call_target="Cholesky" | custom-call | tf_op jit(solution)/shard_map/vmap(jit(cholesky))/cholesky | solution.py:17
  833.5 9.8 %custom-call.76 = f32[1,1,128,128]{2,3,1,0:T(8,128)S(1)} custom-call(f32[1,1,128,128]{3,2,1,0:T(8,128)S(1)} %get-tuple-element.135), custom_call_target="InvertDiagBlocksLowerTriangular" | custom-call | tf_op jit(solution)/shard_map/vmap(jit(cholesky))/cholesky | solution.py:17
  843.8 11.7 %custom-call.77 = f32[1,128,128]{2,1,0:T(8,128)S(1)} custom-call(f32[1,128,128]{2,1,0:T(8,128)S(1)} %fusion.36), custom_call_target="Cholesky" | custom-call | tf_op jit(solution)/shard_map/vmap(jit(cholesky))/cholesky | solution.py:17
  858.3 4.3 while.14
  862.5 19.7 %custom-call.78 = f32[1,2,128,128]{2,3,1,0:T(8,128)S(1)} custom-call(f32[1,2,128,128]{3,2,1,0:T(8,128)S(1)} %bitcast.450), custom_call_target="InvertDiagBlocksLowerTriangular" | custom-call | tf_op jit(solution)/shard_map/vmap(jit(_solve_triangular))/triangular_solve | solution.py:19
  883.8 1.8 collective-permute-start.2
  885.6 7.2 collective-permute-done.2
  893.3 11.7 %custom-call.79 = f32[1,128,128]{2,1,0:T(8,128)S(1)} custom-call(f32[1,128,128]{2,1,0:T(8,128)S(1)} %cholesky.592), custom_call_target="Cholesky" | custom-call | tf_op jit(solution)/shard_map/vmap(jit(cholesky))/cholesky | solution.py:17
  905.1 9.8 %custom-call.80 = f32[1,1,128,128]{2,3,1,0:T(8,128)S(1)} custom-call(f32[1,1,128,128]{3,2,1,0:T(8,128)S(1)} %get-tuple-element.131), custom_call_target="InvertDiagBlocksLowerTriangular" | custom-call | tf_op jit(solution)/shard_map/vmap(jit(cholesky))/cholesky | solution.py:17
  915.4 11.7 %custom-call.81 = f32[1,128,128]{2,1,0:T(8,128)S(1)} custom-call(f32[1,128,128]{2,1,0:T(8,128)S(1)} %fusion.37), custom_call_target="Cholesky" | custom-call | tf_op jit(solution)/shard_map/vmap(jit(cholesky))/cholesky | solution.py:17
  929.9 4.4 while.15
  930.8 1.4 bitcast_dynamic-update-slice_fusion.21
  932.8 1.4 bitcast_dynamic-update-slice_fusion.21
  934.3 19.7 %custom-call.82 = f32[1,2,128,128]{2,3,1,0:T(8,128)S(1)} custom-call(f32[1,2,128,128]{3,2,1,0:T(8,128)S(1)} %bitcast.447), custom_call_target="InvertDiagBlocksLowerTriangular" | custom-call | tf_op jit(solution)/shard_map/vmap(jit(_solve_triangular))/triangular_solve | solution.py:19
  (183 shorter events, 46.5 us)
Async XLA Ops:
  7.2 1.1 copy-start
  7.2 104.2 %copy-start.11 = (s32[4,5]{1,0:T(4,128)S(1)}, s32[4,5]{1,0:T(4,128)}, u32[]{:S(2)}) copy-start(s32[4,5]{1,0:T(4,128)} %param.8) | copy-start | bytes 244
  7.2 104.2 %all-reduce.5.cloned.1.call-start = ((), (), s32[]{:S(2)}) async-start(), calls=%async_computation | async-start | bytes 2097152 | tf_op jit(solution)/shard_map/psum | solution.py:57
  10.6 199.2 %all-gather.2.cloned.1.call-start = ((), (), s32[]{:S(2)}) async-start(), calls=%async_computation.1 | async-start | bytes 17825792 | tf_op jit(solution)/shard_map/all_gather | solution.py:58
  111.5 235.1 %copy-start.10 = (pred[128,128]{1,0:T(8,128)(4,1)}, pred[128,128]{1,0:T(8,128)(4,1)S(1)}, u32[]{:S(2)}) copy-start(pred[128,128]{1,0:T(8,128)(4,1)S(1)} %iota_compare_fusion.5) | copy-start | bytes 49156
  111.6 337.3 %copy-start.9 = (pred[256,256]{1,0:T(8,128)(4,1)}, pred[256,256]{1,0:T(8,128)(4,1)S(1)}, u32[]{:S(2)}) copy-start(pred[256,256]{1,0:T(8,128)(4,1)S(1)} %iota_compare_fusion.2) | copy-start | bytes 196612
  111.8 422.2 %copy-start.6 = (f32[128,256]{1,0:T(8,128)}, f32[128,256]{1,0:T(8,128)S(1)}, u32[]{:S(2)}) copy-start(f32[128,256]{1,0:T(8,128)S(1)} %get-tuple-element.125) | copy-start | bytes 393220
  111.8 422.8 %copy-start.8 = (f32[128,256]{1,0:T(8,128)}, f32[128,256]{1,0:T(8,128)S(1)}, u32[]{:S(2)}) copy-start(f32[128,256]{1,0:T(8,128)S(1)} %get-tuple-element.124) | copy-start | bytes 393220
  283.6 3.2 copy-start.2
  288.3 9.4 copy-start.4
  298.7 1.0 copy-start.3
  454.5 84.0 %copy-start.13 = (s32[2,2]{1,0:T(2,128)}, s32[2,2]{1,0:T(2,128)S(1)}, u32[]{:S(2)}) copy-start(s32[2,2]{1,0:T(2,128)S(1)} %get-tuple-element.442) | copy-start | bytes 52
  538.5 5.7 copy-start.12
  549.2 0.8 copy-start.5
  629.0 51.5 %copy-start.7 = (f32[128,256]{1,0:T(8,128)S(1)}, f32[128,256]{1,0:T(8,128)}, u32[]{:S(2)}) copy-start(f32[128,256]{1,0:T(8,128)} %copy-done.6) | copy-start | bytes 393220
  686.0 37.5 %copy-start.14 = (s32[2,2]{1,0:T(2,128)S(1)}, s32[2,2]{1,0:T(2,128)}, u32[]{:S(2)}) copy-start(s32[2,2]{1,0:T(2,128)} %get-tuple-element.443) | copy-start | bytes 52
  749.1 1.8 collective-permute-start
  813.5 7.7 collective-permute-start.1
  883.8 9.0 collective-permute-start.2
  893.3 62.7 %copy-start.1 = (bf16[1024,256]{1,0:T(8,128)(2,1)S(1)}, bf16[1024,256]{1,0:T(8,128)(2,1)}, u32[]{:S(2)}) copy-start(bf16[1024,256]{1,0:T(8,128)(2,1)} %param.10) | copy-start | bytes 1572868
Sparse Core Ops, SparseCore 0:
  11.8 99.4 all-reduce.4
  113.2 96.5 all-gather.1
where the time goes:
time: 972 us; the launch traced here: 963 us
  other arithmetic  563 us (58%)
  waiting for transfers between devices  215 us (22%)
  local copies, waits for them, and re-layouts  101 us (10%)
  matrix products  60.2 us (6%)
  between operations  20.7 us (2%)
    another operation x45, other arithmetic, cholqr(): low_factor = jnp.linalg.cholesky(gram_matrix)  359 us
    another operation x14, other arithmetic, cholqr(): jax.scipy.linalg.solve_triangular(low_factor, identity, lower=True)  201 us
    psum x1, waiting for transfers between devices, shards(): sketched = lax.psum(partial_sum.astype(jnp.bfloat16), 'col')  101 us
    all_gather x1, waiting for transfers between devices, shards(): all_sketched = lax.all_gather(sketched, 'row', axis=0, tiled=True)  98 us
    reshape x1, local copies, waits for them, and re-layouts, off_products(): all_sketched.reshape(leaf_total, front_blocks.shape[2], all_sketched.shap...  22.4 us
  transfers between devices with their start and end apart: 5, of which 5 were waited for; matrix products, arithmetic and copies ran while one was open for 0% of the time, Pallas kernels for 0%

commit v1 on v0

--- a/solution.py
+++ b/solution.py
@@ -55,7 +55,9 @@
     )
     partial_sum = jnp.dot(samples, local_rows, preferred_element_type=jnp.float32)
     sketched = lax.psum(partial_sum.astype(jnp.bfloat16), "col")
-    all_sketched = lax.all_gather(sketched, "row", axis=0, tiled=True)
+    all_sketched = jnp.concatenate(
+        lax.all_to_all(jnp.stack([sketched] * lax.axis_size("row")), "row", 0, 0), axis=0
+    )
     off_samples = off_products(all_sketched, front_blocks, block_cols, leaf_ids, top_level)
     leaf_basis = jax.vmap(cholqr)(off_samples[:, 0].astype(jnp.float32))
     carried = jnp.einsum(

time: 972 us -> 1230 us (1.27)
  waiting for transfers between devices: 215 us -> 478 us
  local copies, waits for them, and re-layouts: 101 us -> 86.4 us
    all_to_all x0 -> x1, waiting for transfers between devices: none -> 363 us  [shards(): lax.all_to_all(jnp.stack([sketched] * lax.axis_size('row')), 'row', 0, 0)]
    all_gather x1 -> x0, waiting for transfers between devices: 98 us -> none  [shards(): all_sketched = lax.all_gather(sketched, 'row', axis=0, tiled=True)]
    reshape x1 -> x0, local copies, waits for them, and re-layouts: 22.4 us -> none  [off_products(): all_sketched.reshape(leaf_total, front_blocks.shape[2], all_sketched.shap...]
where the time goes in v1:
time: 1230 us; the launch traced here: 1220 us
  other arithmetic  563 us (46%)
  waiting for transfers between devices  478 us (39%)
  local copies, waits for them, and re-layouts  86.4 us (7%)
  matrix products  60.2 us (5%)
  between operations  20.7 us (2%)
  starting transfers between devices  13.2 us (1%)
    all_to_all x1, waiting for transfers between devices, shards(): lax.all_to_all(jnp.stack([sketched] * lax.axis_size('row')), 'row', 0, 0)  363 us
    another operation x45, other arithmetic, cholqr(): low_factor = jnp.linalg.cholesky(gram_matrix)  359 us
    another operation x14, other arithmetic, cholqr(): jax.scipy.linalg.solve_triangular(low_factor, identity, lower=True)  201 us
    psum x1, waiting for transfers between devices, shards(): sketched = lax.psum(partial_sum.astype(jnp.bfloat16), 'col')  101 us
  transfers between devices with their start and end apart: 5, of which 5 were waited for; matrix products, arithmetic and copies ran while one was open for 0% of the time, Pallas kernels for 0%

profile of v1, /device:TPU:1, one launch (start us, length us, event | category | flops | bytes accessed | tf_op | source)
XLA Modules:
  0.0 1222.4 jit_solution(9506933671621273931)
XLA Ops:
  8.2 2.4 fusion.2
  10.6 100.7 %all-reduce.5.cloned.1.call-done = bf16[2048,256]{0,1:T(8,128)(2,1)} async-done(((bf16[2048,256]{0,1:T(8,128)(2,1)}), bf16[2048,256]{0,1:T(8,128)(2,1)}) %all-reduce.5.cloned.1.call-update) | async-done | bytes 1048592 | tf_op jit(solution)/shard_map/psum | solution.py:57
  111.3 1.5 copy.94
  112.8 5.9 stack.2
  118.8 9.3 all-to-all-start
  128.5 362.8 %all-to-all-done = bf16[16,2048,256]{2,1,0:T(8,128)(2,1)} async-done(((bf16[16,2048,256]{2,1,0:T(8,128)(2,1)}), bf16[16,2048,256]{2,1,0:T(8,128)(2,1)}, u32[]{:S(2)}, u32[]{:S(2)}) %all-to-all-start) | async-done | bytes 16777248 | tf_op jit(solution)/shard_map/all_to_all | solution.py:59
  491.3 9.9 gather_fusion
  501.3 12.5 %convolution_bitcast_fusion = f32[4,5,512,256]{2,3,1,0:T(8,128)} fusion(bf16[4,5,512,256]{3,2,1,0:T(8,128)(2,1)} %bitcast.432, bf16[4,5,512,512]{3,2,1,0:T(8,128)(2,1)} %param.7), kind=kOutput, calls=%fused_computation.17 | convolution fusion | flops 2684354560 | bytes 26214400 | tf_op jit(solution)/shard_map/nkab,nkbc->nkac/dot_general | solution.py:29
  513.8 17.1 %copy.96 = f32[4,5,512,256]{3,1,2,0:T(8,128)} copy(f32[4,5,512,256]{2,3,1,0:T(8,128)} %convolution_bitcast_fusion) | data formatting | bytes 20971520 | tf_op jit(solution)/shard_map/nkab,nkbc->nkac/dot_general | solution.py:29
  530.9 11.9 convolution_convert_fusion
  542.8 3.2 copy-done.2
  546.0 1.4 slice.234
  547.5 9.4 slice.235
  558.9 46.9 %custom-call.47 = f32[4,128,128]{2,1,0:T(8,128)S(1)} custom-call(f32[4,128,128]{2,1,0:T(8,128)S(1)} %cholesky.577), custom_call_target="Cholesky" | custom-call | tf_op jit(solution)/shard_map/vmap(jit(cholesky))/cholesky | solution.py:17
  605.9 39.3 %custom-call.48 = f32[4,1,128,128]{2,3,1,0:T(8,128)S(1)} custom-call(f32[4,1,128,128]{3,2,1,0:T(8,128)S(1)} %select_bitcast_fusion), custom_call_target="InvertDiagBlocksLowerTriangular" | custom-call | tf_op jit(solution)/shard_map/vmap(jit(cholesky))/cholesky | solution.py:17
  645.3 1.4 constant_dynamic-update-slice_fusion.7
  646.7 1.6 convolution_subtract_fusion.2
  648.3 59.6 %custom-call.49 = f32[4,128,128]{2,1,0:T(8,128)S(1)} custom-call(f32[4,128,128]{2,1,0:T(8,128)S(1)} %convolution_subtract_fusion.2), custom_call_target="Cholesky" | custom-call | tf_op jit(solution)/shard_map/vmap(jit(cholesky))/cholesky | solution.py:17
  708.4 5.3 while.10
  709.0 2.1 bitcast_dynamic-update-slice_fusion.16
  711.7 2.1 bitcast_dynamic-update-slice_fusion.16
  713.7 79.4 %custom-call.50 = f32[4,2,128,128]{2,3,1,0:T(8,128)S(1)} custom-call(f32[4,2,128,128]{3,2,1,0:T(8,128)} %bitcast.450), custom_call_target="InvertDiagBlocksLowerTriangular" | custom-call | tf_op jit(solution)/shard_map/vmap(jit(_solve_triangular))/triangular_solve | solution.py:19
  795.1 2.7 multiply_convert_fusion.2
  797.8 5.7 multiply_convert_fusion
  805.1 2.1 copy.109
  809.9 24.3 %custom-call.51 = f32[2,128,128]{2,1,0:T(8,128)S(1)} custom-call(f32[2,128,128]{2,1,0:T(8,128)} %cholesky.580), custom_call_target="Cholesky" | custom-call | tf_op jit(solution)/shard_map/vmap(jit(cholesky))/cholesky | solution.py:17
  834.2 1.4 select_bitcast_fusion.1
  836.4 21.5 %custom-call.52 = f32[2,1,128,128]{2,3,1,0:T(8,128)} custom-call(f32[2,1,128,128]{3,2,1,0:T(8,128)} %select_bitcast_fusion.1), custom_call_target="InvertDiagBlocksLowerTriangular" | custom-call | tf_op jit(solution)/shard_map/vmap(jit(cholesky))/cholesky | solution.py:17
  857.9 1.9 constant_dynamic-update-slice_fusion.5
  859.8 1.9 convolution_subtract_fusion.3
  861.7 24.9 %custom-call.53 = f32[2,128,128]{2,1,0:T(8,128)} custom-call(f32[2,128,128]{2,1,0:T(8,128)} %convolution_subtract_fusion.3), custom_call_target="Cholesky" | custom-call | tf_op jit(solution)/shard_map/vmap(jit(cholesky))/cholesky | solution.py:17
  886.6 1.6 select_reduce_fusion.2
  888.5 2.0 select_select_fusion.1
  890.5 8.3 while.11
  891.7 3.0 bitcast_dynamic-update-slice_fusion.17
  895.9 2.9 bitcast_dynamic-update-slice_fusion.17
  898.8 40.9 %custom-call.54 = f32[2,2,128,128]{2,3,1,0:T(8,128)} custom-call(f32[2,2,128,128]{3,2,1,0:T(8,128)} %bitcast.451), custom_call_target="InvertDiagBlocksLowerTriangular" | custom-call | tf_op jit(solution)/shard_map/vmap(jit(_solve_triangular))/triangular_solve | solution.py:19
  945.8 11.7 custom-call.67
  957.6 9.8 custom-call.68
  967.9 12.1 custom-call.69
  982.8 4.1 while.12
  983.4 1.4 bitcast_dynamic-update-slice_fusion.18
  985.5 1.4 bitcast_dynamic-update-slice_fusion.18
  986.9 19.7 %custom-call.70 = f32[1,2,128,128]{2,3,1,0:T(8,128)S(1)} custom-call(f32[1,2,128,128]{3,2,1,0:T(8,128)S(1)} %bitcast.447), custom_call_target="InvertDiagBlocksLowerTriangular" | custom-call | tf_op jit(solution)/shard_map/vmap(jit(_solve_triangular))/triangular_solve | solution.py:19
  1011.2 11.7 custom-call.71
  1022.9 9.8 custom-call.72
  1033.2 11.7 custom-call.73
  1047.6 4.2 while.13
  1051.9 19.7 %custom-call.74 = f32[1,2,128,128]{2,3,1,0:T(8,128)S(1)} custom-call(f32[1,2,128,128]{3,2,1,0:T(8,128)S(1)} %bitcast.448), custom_call_target="InvertDiagBlocksLowerTriangular" | custom-call | tf_op jit(solution)/shard_map/vmap(jit(_solve_triangular))/triangular_solve | solution.py:19
  1074.0 6.9 collective-permute-done.1
  1081.4 11.7 custom-call.75
  1093.1 9.8 custom-call.76
  1103.4 11.7 custom-call.77
  1117.8 4.3 while.14
  1122.1 19.7 %custom-call.78 = f32[1,2,128,128]{2,3,1,0:T(8,128)S(1)} custom-call(f32[1,2,128,128]{3,2,1,0:T(8,128)S(1)} %bitcast.449), custom_call_target="InvertDiagBlocksLowerTriangular" | custom-call | tf_op jit(solution)/shard_map/vmap(jit(_solve_triangular))/triangular_solve | solution.py:19
  1143.4 2.2 collective-permute-start.2
  1145.6 6.4 collective-permute-done.2
  1152.5 11.7 custom-call.79
  1164.3 9.8 custom-call.80
  1174.6 11.7 custom-call.81
  1189.1 4.4 while.15
  1190.0 1.4 bitcast_dynamic-update-slice_fusion.21
  1192.0 1.4 bitcast_dynamic-update-slice_fusion.21
  1193.5 19.7 %custom-call.82 = f32[1,2,128,128]{2,3,1,0:T(8,128)S(1)} custom-call(f32[1,2,128,128]{3,2,1,0:T(8,128)S(1)} %bitcast.446), custom_call_target="InvertDiagBlocksLowerTriangular" | custom-call | tf_op jit(solution)/shard_map/vmap(jit(_solve_triangular))/triangular_solve | solution.py:19
  (183 shorter events, 50.4 us)
Async XLA Ops:
  7.2 1.1 copy-start
  7.2 104.2 %all-reduce.5.cloned.1.call-start = ((), (), s32[]{:S(2)}) async-start(), calls=%async_computation.1 | async-start | bytes 2097152 | tf_op jit(solution)/shard_map/psum | solution.py:57
  118.7 9.4 copy-start.11
  118.8 372.6 %all-to-all-start = ((bf16[16,2048,256]{2,1,0:T(8,128)(2,1)}), bf16[16,2048,256]{2,1,0:T(8,128)(2,1)}, u32[]{:S(2)}, u32[]{:S(2)}) async-start(bf16[16,2048,256]{2,1,0:T(8,128)(2,1)} %stack.2), calls=%async_computation | async-start | bytes 33554432 | tf_op jit(solution)/shard_map/all_to_all | solution.py:59
  128.2 477.6 %copy-start.10 = (pred[128,128]{1,0:T(8,128)(4,1)}, pred[128,128]{1,0:T(8,128)(4,1)S(1)}, u32[]{:S(2)}) copy-start(pred[128,128]{1,0:T(8,128)(4,1)S(1)} %iota_compare_fusion.5) | copy-start | bytes 49156
  128.3 579.8 %copy-start.9 = (pred[256,256]{1,0:T(8,128)(4,1)}, pred[256,256]{1,0:T(8,128)(4,1)S(1)}, u32[]{:S(2)}) copy-start(pred[256,256]{1,0:T(8,128)(4,1)S(1)} %iota_compare_fusion.2) | copy-start | bytes 196612
  128.5 664.7 %copy-start.6 = (f32[128,256]{1,0:T(8,128)}, f32[128,256]{1,0:T(8,128)S(1)}, u32[]{:S(2)}) copy-start(f32[128,256]{1,0:T(8,128)S(1)} %get-tuple-element.125) | copy-start | bytes 393220
  128.5 665.3 %copy-start.8 = (f32[128,256]{1,0:T(8,128)}, f32[128,256]{1,0:T(8,128)S(1)}, u32[]{:S(2)}) copy-start(f32[128,256]{1,0:T(8,128)S(1)} %get-tuple-element.124) | copy-start | bytes 393220
  542.8 3.2 copy-start.2
  547.5 9.4 copy-start.4
  558.0 1.0 copy-start.3
  713.7 84.0 %copy-start.13 = (s32[2,2]{1,0:T(2,128)}, s32[2,2]{1,0:T(2,128)S(1)}, u32[]{:S(2)}) copy-start(s32[2,2]{1,0:T(2,128)S(1)} %get-tuple-element.440) | copy-start | bytes 52
  797.7 5.7 copy-start.12
  808.4 0.8 copy-start.5
  888.2 51.5 %copy-start.7 = (f32[128,256]{1,0:T(8,128)S(1)}, f32[128,256]{1,0:T(8,128)}, u32[]{:S(2)}) copy-start(f32[128,256]{1,0:T(8,128)} %copy-done.6) | copy-start | bytes 393220
  945.3 37.5 %copy-start.14 = (s32[2,2]{1,0:T(2,128)S(1)}, s32[2,2]{1,0:T(2,128)}, u32[]{:S(2)}) copy-start(s32[2,2]{1,0:T(2,128)} %get-tuple-element.441) | copy-start | bytes 52
  1008.3 2.3 collective-permute-start
  1073.3 7.6 collective-permute-start.1
  1143.4 8.6 collective-permute-start.2
  1152.4 62.7 %copy-start.1 = (bf16[1024,256]{1,0:T(8,128)(2,1)S(1)}, bf16[1024,256]{1,0:T(8,128)(2,1)}, u32[]{:S(2)}) copy-start(bf16[1024,256]{1,0:T(8,128)(2,1)} %param.10) | copy-start | bytes 1572868
Sparse Core Ops, SparseCore 0:
  11.8 99.4 all-reduce.4
